TPU v7x, 32 devices: a whole 2x2x4 slice. The times are simulated.
32 devices in a mesh: dp: 4 (over x, core), fsdp: 8 (over z, y).
Axes of the slice: x: 2, y: 2, z: 4, core: 2. Of those that a mesh axis runs over, the one named last changes fastest.
Arguments:
- mel_clips: bfloat16 [640, 256, 512], P(('dp', 'fsdp')), may hold values from -6 to 6
- live_counts: int32 [32, 4], P(('dp', 'fsdp')), may hold values from 1 to 5, as said below
- conv_weight: bfloat16 [512, 7], P(('dp', 'fsdp')), may hold values from -2 to 2
- conv_bias: bfloat16 [512], P(('dp', 'fsdp')), may hold values from -3 to 3
- norm_gain: bfloat16 [512], P(('dp', 'fsdp')), may hold values from 0.25 to 1.75
- norm_shift: bfloat16 [512], P(('dp', 'fsdp')), may hold values from -2 to 2
- in_weight: bfloat16 [512, 1536], P(('dp', 'fsdp')), may hold values from -0.25 to 0.25
- in_bias: bfloat16 [1536], P(('dp', 'fsdp')), may hold values from -2 to 2
- out_weight: bfloat16 [1536, 512], P(('dp', 'fsdp')), may hold values from -0.3125 to 0.3125
- out_bias: bfloat16 [512], P(('dp', 'fsdp')), may hold values from -2 to 2
- layer_scale: bfloat16 [512], P(('dp', 'fsdp')), may hold values from 0.29882812 to 1.1953125
- cotangent: bfloat16 [640, 256, 512], P(('dp', 'fsdp')), may hold values from -6 to 6
Outputs:
- block_out: bfloat16 [640, 256, 512], P(('dp', 'fsdp'))
- grad_clips: bfloat16 [640, 256, 512], P(('dp', 'fsdp'))
- grad_conv_weight: float32 [512, 7], P(('dp', 'fsdp'))
- grad_conv_bias: float32 [512], P(('dp', 'fsdp'))
- grad_norm_gain: float32 [512], P(('dp', 'fsdp'))
- grad_norm_shift: float32 [512], P(('dp', 'fsdp'))
- grad_in_weight: float32 [512, 1536], P(('dp', 'fsdp'))
- grad_in_bias: float32 [1536], P(('dp', 'fsdp'))
- grad_out_weight: float32 [1536, 512], P(('dp', 'fsdp'))
- grad_out_bias: float32 [512], P(('dp', 'fsdp'))
- grad_layer_scale: float32 [512], P(('dp', 'fsdp'))
Inputs may be any that keep to these rules, and one draw needn't show every extreme that they name: Slot s of micro-batch m on device d holds a live clip when s < live_counts[d, m]; some device has all 5 slots live in some micro-batch, and some device only one.
All inputs are finite; a program needn't handle non-finite values.
Results may differ from a plain program's by a relative error of at most 0.0063.
Values may be sent and summed in bfloat16 or wider, within the bound.
A program may use at most 256 MiB of HBM per device.

v0:
```python
from functools import partial

import jax
import jax.numpy as jnp
from jax import lax
from jax.sharding import PartitionSpec as P


def conv_norm(mel_block, conv_weight, conv_bias, norm_gain, norm_shift):
    frames = mel_block.shape[1]
    kernel = conv_weight.shape[1]
    margin = (kernel - 1) // 2
    padded = jnp.pad(mel_block, ((0, 0), (margin, margin), (0, 0)))
    mixed_sum = conv_bias + padded[:, 0:frames, :] * conv_weight[:, 0]
    for offset in range(1, kernel):
        mixed_sum = mixed_sum + padded[:, offset : offset + frames, :] * conv_weight[:, offset]
    center = mixed_sum - jnp.mean(mixed_sum, axis=-1, keepdims=True)
    spread = jnp.mean(center * center, axis=-1, keepdims=True)
    return center * lax.rsqrt(spread + 1e-06) * norm_gain + norm_shift


def contract_rows(left_side, right_side):
    return lax.dot_general(
        left_side, right_side, (((0,), (0,)), ((), ())), preferred_element_type=jnp.float32
    )


def contract_last(left_side, right_side):
    return lax.dot_general(
        left_side, right_side, (((1,), (1,)), ((), ())), preferred_element_type=jnp.float32
    )


def on_device(
    mel_clips,
    live_counts,
    conv_weight,
    conv_bias,
    norm_gain,
    norm_shift,
    in_weight,
    in_bias,
    out_weight,
    out_bias,
    layer_scale,
    cotangent,
):
    shards = (
        conv_weight,
        conv_bias,
        norm_gain,
        norm_shift,
        in_weight,
        in_bias,
        out_weight,
        out_bias,
        layer_scale,
    )
    micro_count = live_counts.shape[1]
    slot_count = mel_clips.shape[0] // micro_count
    channels = mel_clips.shape[2]
    devices = lax.axis_size(("dp", "fsdp"))
    totals = tuple(
        (jnp.zeros((piece.shape[0] * devices,) + piece.shape[1:], jnp.float32) for piece in shards)
    )
    block_outs = []
    block_grads = []
    for micro_step in range(micro_count):
        forward_set = (
            lax.all_gather(conv_weight, ("dp", "fsdp"), axis=0, tiled=True),
            lax.all_gather(conv_bias, ("dp", "fsdp"), axis=0, tiled=True),
            lax.all_gather(norm_gain, ("dp", "fsdp"), axis=0, tiled=True),
            lax.all_gather(norm_shift, ("dp", "fsdp"), axis=0, tiled=True),
            lax.all_gather(in_weight, ("dp", "fsdp"), axis=0, tiled=True),
            lax.all_gather(in_bias, ("dp", "fsdp"), axis=0, tiled=True),
            lax.all_gather(out_weight, ("dp", "fsdp"), axis=0, tiled=True),
            lax.all_gather(out_bias, ("dp", "fsdp"), axis=0, tiled=True),
            lax.all_gather(layer_scale, ("dp", "fsdp"), axis=0, tiled=True),
        )
        (
            full_conv,
            full_cbias,
            full_gain,
            full_shift,
            full_in,
            full_ibias,
            full_out,
            full_obias,
            full_scale,
        ) = forward_set
        clip_block = mel_clips[micro_step * slot_count : (micro_step + 1) * slot_count].astype(
            jnp.float32
        )
        live_mask = (lax.iota(jnp.int32, slot_count) < live_counts[0, micro_step]).astype(
            jnp.float32
        )
        normed, norm_pull = jax.vjp(
            conv_norm,
            clip_block,
            full_conv.astype(jnp.float32),
            full_cbias.astype(jnp.float32),
            full_gain.astype(jnp.float32),
            full_shift.astype(jnp.float32),
        )
        rows_low = normed.reshape(-1, channels).astype(jnp.bfloat16)
        hidden = jnp.dot(rows_low, full_in, preferred_element_type=jnp.float32) + full_ibias.astype(
            jnp.float32
        )
        active, gelu_pull = jax.vjp(partial(jax.nn.gelu, approximate=False), hidden)
        active_low = active.astype(jnp.bfloat16)
        output = jnp.dot(
            active_low, full_out, preferred_element_type=jnp.float32
        ) + full_obias.astype(jnp.float32)
        output = output.reshape(clip_block.shape)
        scale_full = full_scale.astype(jnp.float32)
        branch = output * scale_full * live_mask[:, None, None]
        block_outs.append((clip_block + branch).astype(jnp.bfloat16))
        back_in, back_out, scale_back = (
            lax.all_gather(in_weight, ("dp", "fsdp"), axis=0, tiled=True),
            lax.all_gather(out_weight, ("dp", "fsdp"), axis=0, tiled=True),
            lax.all_gather(layer_scale, ("dp", "fsdp"), axis=0, tiled=True),
        )
        back_scale = scale_back.astype(jnp.float32)
        grad_out = cotangent[micro_step * slot_count : (micro_step + 1) * slot_count].astype(
            jnp.float32
        )
        masked_out = grad_out * live_mask[:, None, None]
        grad_scale = jnp.sum((masked_out * output).reshape(-1, channels), axis=0)
        grad_output = (masked_out * back_scale).reshape(-1, channels).astype(jnp.bfloat16)
        grad_obias = jnp.sum(grad_output.astype(jnp.float32), axis=0)
        grad_wout = contract_rows(active_low, grad_output)
        grad_active = contract_last(grad_output, back_out)
        (grad_hidden,) = gelu_pull(grad_active)
        hidden_low = grad_hidden.astype(jnp.bfloat16)
        grad_ibias = jnp.sum(hidden_low.astype(jnp.float32), axis=0)
        grad_win = contract_rows(rows_low, hidden_low)
        grad_normed = contract_last(hidden_low, back_in)
        grad_input, grad_conv, grad_cbias, grad_gain, grad_shift = norm_pull(
            grad_normed.reshape(clip_block.shape)
        )
        block_grads.append((grad_out + grad_input).astype(jnp.bfloat16))
        parts_now = (
            grad_conv,
            grad_cbias,
            grad_gain,
            grad_shift,
            grad_win,
            grad_ibias,
            grad_wout,
            grad_obias,
            grad_scale,
        )
        totals = tuple((a + b for a, b in zip(totals, parts_now)))
    grad_sums = (
        lax.psum_scatter(totals[0], ("dp", "fsdp"), scatter_dimension=0, tiled=True),
        lax.psum_scatter(totals[1], ("dp", "fsdp"), scatter_dimension=0, tiled=True),
        lax.psum_scatter(totals[2], ("dp", "fsdp"), scatter_dimension=0, tiled=True),
        lax.psum_scatter(totals[3], ("dp", "fsdp"), scatter_dimension=0, tiled=True),
        lax.psum_scatter(totals[4], ("dp", "fsdp"), scatter_dimension=0, tiled=True),
        lax.psum_scatter(totals[5], ("dp", "fsdp"), scatter_dimension=0, tiled=True),
        lax.psum_scatter(totals[6], ("dp", "fsdp"), scatter_dimension=0, tiled=True),
        lax.psum_scatter(totals[7], ("dp", "fsdp"), scatter_dimension=0, tiled=True),
        lax.psum_scatter(totals[8], ("dp", "fsdp"), scatter_dimension=0, tiled=True),
    )
    block_out = jnp.concatenate(block_outs, axis=0)
    grad_clips = jnp.concatenate(block_grads, axis=0)
    return (
        block_out,
        grad_clips,
        grad_sums[0],
        grad_sums[1],
        grad_sums[2],
        grad_sums[3],
        grad_sums[4],
        grad_sums[5],
        grad_sums[6],
        grad_sums[7],
        grad_sums[8],
    )


def solution(mesh):
    in_specs = (
        P(("dp", "fsdp"), None, None),
        P(("dp", "fsdp"), None),
        P(("dp", "fsdp"), None),
        P(("dp", "fsdp")),
        P(("dp", "fsdp")),
        P(("dp", "fsdp")),
        P(("dp", "fsdp"), None),
        P(("dp", "fsdp")),
        P(("dp", "fsdp"), None),
        P(("dp", "fsdp")),
        P(("dp", "fsdp")),
        P(("dp", "fsdp"), None, None),
    )
    out_specs = (
        P(("dp", "fsdp"), None, None),
        P(("dp", "fsdp"), None, None),
        P(("dp", "fsdp"), None),
        P(("dp", "fsdp")),
        P(("dp", "fsdp")),
        P(("dp", "fsdp")),
        P(("dp", "fsdp"), None),
        P(("dp", "fsdp")),
        P(("dp", "fsdp"), None),
        P(("dp", "fsdp")),
        P(("dp", "fsdp")),
    )
    return jax.shard_map(
        on_device, mesh=mesh, in_specs=in_specs, out_specs=out_specs, check_vma=False
    )
```

profile of v0, /device:TPU:0, one launch (start us, length us, event | category | flops | bytes accessed | tf_op | source)
XLA Modules:
  0.0 748.2 jit_solution(5183348924312344757)
XLA Ops:
  8.0 0.7 all-gather.6.cloned.1.call-update
  8.7 0.9 dynamic-update-slice
  9.6 0.8 dynamic-update-slice.1
  10.4 0.8 dynamic-update-slice.2
  11.3 0.8 dynamic-update-slice.4
  12.1 0.8 dynamic-update-slice.5
  13.0 0.8 dynamic-update-slice.3
  13.8 42.2 %all-reduce.73 = (bf16[512]{0:T(512)(128)(2,1)S(1)}, bf16[512]{0:T(512)(128)(2,1)S(1)}, bf16[512]{0:T(512)(128)(2,1)S(1)}, bf16[1536]{0:T(1024)(128)(2,1)S(1)}, ...) all-reduce(bf16[512]{0:T(512)(128)(2,1)S(1)} %dynamic-update-slice,, ...), channel_id=1, replica_groups=mesh['dp'=4,'fsdp'=8] {'dp','fsdp'}, use_global_device_ids=true, to_apply=%add.60 | all-reduce | flops 4096 | bytes 16384
  56.0 66.8 %all-gather = bf16[32,16,7]{1,2,0:T(8,128)(2,1)S(1)} all-gather(bf16[1,16,7]{1,2,0:T(8,128)(2,1)} %bitcast.200), channel_id=1, replica_groups=mesh['dp'=4,'fsdp'=8] {'dp','fsdp'}, dimensions={0}, use_global_device_ids=true | all-gather | bytes 7392 | tf_op jit(solution)/shard_map/all_gather | solution.py:70
  123.2 7.1 slice_convert_fusion.3
  130.4 28.4 %fusion.61 = (f32[5,256]{1,0:T(8,128)S(1)}, f32[5,256,512]{2,1,0:T(8,128)S(1)}, f32[5,256]{1,0:T(8,128)S(1)}, f32[5,256,512]{2,1,0:T(8,128)S(1)}, f32[5,256]{1,0...) fusion(f32[512]{0:T(512)S(1)} %bitcast.152, f32[512]{0:T(512)S(1)} %bitcast.143, ...), kind=kLoop, calls=%fused_computation.295 | loop fusion | flops 39316480 | bytes 21008384 | tf_op jit(solution)/shard_map/jvp()/reduce_sum | solution.py:17
  158.8 0.9 multiply_reduce_fusion.36
  159.8 1.0 copy-done.58
  160.9 0.9 multiply_reduce_fusion.38
  161.8 0.8 copy-done.60
  163.9 1.8 compare_convert_fusion
  165.7 1.8 compare_convert_fusion.2
  167.6 3.7 add_convert_fusion.11
  171.3 22.9 %multiply_convert_fusion.2 = (bf16[1280,1536]{1,0:T(8,128)(2,1)}, f32[1280,1536]{1,0:T(8,128)}, f32[1280,1536]{1,0:T(8,128)}) fusion(f32[1536]{0:T(1024)S(1)} %convert_element_type.238, bf16[1280,512]{1,0:T(8,128)(2,1)} %bitcast.129, bf16[512,1536]{1,0:T(8,128)(2,1)} %all-gather.4.cloned.1.call-done), kind=kOutput, calls=%fused_computation.46 | convolution fusion | flops 2143027200 | bytes 22550528 | tf_op jit(solution)/shard_map/dot_general | solution.py:106
  194.2 20.6 %multiply_convert_fusion = (bf16[1280,1536]{1,0:T(8,128)(2,1)}, f32[1280,1536]{1,0:T(8,128)}, f32[1280,1536]{1,0:T(8,128)}) fusion(f32[1536]{0:T(1024)S(1)} %convert_element_type.238, bf16[1280,512]{1,0:T(8,128)(2,1)S(1)} %bitcast.125, bf16[512,1536]{1,0:T(8,128)(2,1)S(1)} %copy-done.86), kind=kOutput, calls=%fused_computation.20 | convolution fusion | flops 2143027200 | bytes 22550528 | tf_op jit(solution)/shard_map/dot_general | solution.py:106
  214.8 5.0 convolution_add_fusion.6
  219.8 2.2 convolution_add_fusion.4
  222.1 20.4 %multiply_convert_fusion.3 = (bf16[1280,1536]{1,0:T(8,128)(2,1)S(1)}, f32[1280,1536]{1,0:T(8,128)}, f32[1280,1536]{1,0:T(8,128)}) fusion(f32[1536]{0:T(1024)S(1)} %convert_element_type.238, bf16[1280,512]{1,0:T(8,128)(2,1)S(1)} %bitcast.133, bf16[512,1536]{1,0:T(8,128)(2,1)S(1)} %copy-done.86), kind=kOutput, calls=%fused_computation.59 | convolution fusion | flops 2143027200 | bytes 22550528 | tf_op jit(solution)/shard_map/dot_general | solution.py:106
  242.4 2.2 convolution_add_fusion.7
  244.7 20.4 %multiply_convert_fusion.1 = (bf16[1280,1536]{1,0:T(8,128)(2,1)S(1)}, f32[1280,1536]{1,0:T(8,128)}, f32[1280,1536]{1,0:T(8,128)}) fusion(f32[1536]{0:T(1024)S(1)} %convert_element_type.238, bf16[1280,512]{1,0:T(8,128)(2,1)S(1)} %bitcast.127, bf16[512,1536]{1,0:T(8,128)(2,1)S(1)} %copy-done.86), kind=kOutput, calls=%fused_computation.33 | convolution fusion | flops 2143027200 | bytes 22550528 | tf_op jit(solution)/shard_map/dot_general | solution.py:106
  265.1 2.2 convolution_add_fusion.5
  267.4 2.2 slice-done.2
  269.9 5.0 add_convert_fusion.10
  275.0 7.4 fusion.75
  282.4 7.8 %convert_reduce_fusion = (f32[1536]{0:T(1024)S(1)}, bf16[1280,1536]{1,0:T(8,128)(2,1)S(1)}) fusion(f32[1280,1536]{1,0:T(8,128)} %get-tuple-element.102, f32[1280,1536]{1,0:T(8,128)} %get-tuple-element.205, bf16[1280,512]{1,0:T(8,128)(2,1)S(1)} %bitcast.135, bf16[1536,512]{1,0:T(8,128)(2,1)S(1)} %copy-done.88), kind=kOutput, calls=%fused_computation.12 | convolution fusion | flops 2044721664 | bytes 22550528 | tf_op jit(solution)/shard_map/dot_general | solution.py:29
  290.3 2.2 fusion.70
  292.5 0.9 copy-done.7
  293.4 0.9 multiply_reduce_fusion
  294.4 7.8 %convert_reduce_fusion.2 = (f32[1536]{0:T(1024)S(1)}, bf16[1280,1536]{1,0:T(8,128)(2,1)S(1)}) fusion(f32[1280,1536]{1,0:T(8,128)} %get-tuple-element.94, f32[1280,1536]{1,0:T(8,128)} %get-tuple-element.207, bf16[1280,512]{1,0:T(8,128)(2,1)S(1)} %bitcast.139, bf16[1536,512]{1,0:T(8,128)(2,1)S(1)} %copy-done.88), kind=kOutput, calls=%fused_computation.14 | convolution fusion | flops 2044721664 | bytes 22550528 | tf_op jit(solution)/shard_map/dot_general | solution.py:29
  302.2 2.2 fusion.73
  304.4 8.2 %convert_reduce_fusion.1 = (f32[1536]{0:T(1024)S(1)}, bf16[1280,1536]{1,0:T(8,128)(2,1)S(1)}) fusion(f32[1280,1536]{1,0:T(8,128)} %get-tuple-element.98, f32[1280,1536]{1,0:T(8,128)} %get-tuple-element.204, bf16[1280,512]{1,0:T(8,128)(2,1)S(1)} %bitcast.137, bf16[1536,512]{1,0:T(8,128)(2,1)S(1)} %copy-done.88), kind=kOutput, calls=%fused_computation.13 | convolution fusion | flops 2044721664 | bytes 22550528 | tf_op jit(solution)/shard_map/dot_general | solution.py:29
  312.7 2.2 fusion.71
  314.9 9.1 %convert_reduce_fusion.3 = (f32[1536]{0:T(1024)S(1)}, bf16[1280,1536]{1,0:T(8,128)(2,1)}) fusion(f32[1280,1536]{1,0:T(8,128)} %get-tuple-element.90, f32[1280,1536]{1,0:T(8,128)} %get-tuple-element.206, bf16[1280,512]{1,0:T(8,128)(2,1)S(1)} %bitcast.142, bf16[1536,512]{1,0:T(8,128)(2,1)S(1)} %copy-done.88), kind=kOutput, calls=%fused_computation.15 | convolution fusion | flops 2044721664 | bytes 22550528 | tf_op jit(solution)/shard_map/dot_general | solution.py:29
  324.1 4.6 fusion.72
  328.8 3.9 multiply_reduce_fusion.3
  332.8 4.4 fusion.56
  337.4 8.0 %multiply_reduce_fusion.31 = (f32[512]{0:T(512)S(1)}, f32[512]{0:T(512)S(1)}, f32[512]{0:T(512)S(1)}, f32[512]{0:T(512)S(1)}, f32[512]{0:T(512)S(1)}, /*index=5*...) fusion(f32[5,256,512]{2,1,0:T(8,128)S(1)} %copy-done.11, ...), kind=kLoop, calls=%fused_computation.179 | loop fusion | flops 13758976 | bytes 23626752 | tf_op jit(solution)/shard_map/transpose(jvp())/reduce_sum | solution.py:16
  345.3 18.9 %multiply_reduce_fusion.17 = (f32[512]{0:T(512)S(1)}, f32[512]{0:T(512)S(1)}, f32[512]{0:T(512)S(1)}, f32[512]{0:T(512)S(1)}, f32[512]{0:T(512)S(1)}, /*index=5*...) fusion(f32[5,256,512]{2,1,0:T(8,128)} %get-tuple-element.138, ...), kind=kLoop, calls=%fused_computation.165 | loop fusion | flops 17691648 | bytes 41979904 | tf_op jit(solution)/shard_map/transpose(jvp())/reduce_sum | solution.py:16
  364.2 15.1 %multiply_reduce_fusion.28 = (f32[512]{0:T(512)S(1)}, f32[512]{0:T(512)S(1)}, f32[512]{0:T(512)S(1)}, f32[512]{0:T(512)S(1)}, f32[512]{0:T(512)S(1)}, /*index=5*...) fusion(bf16[20,256,512]{2,1,0:T(8,128)(2,1)} %param.12, ...), kind=kLoop, calls=%fused_computation.176 | loop fusion | flops 20964864 | bytes 21020672 | tf_op jit(solution)/shard_map/transpose(jvp())/reduce_sum | solution.py:16
  379.4 8.0 %multiply_reduce_fusion.24 = (f32[512]{0:T(512)S(1)}, f32[512]{0:T(512)S(1)}, f32[512]{0:T(512)S(1)}, f32[512]{0:T(512)S(1)}, f32[512]{0:T(512)S(1)}, /*index=5*...) fusion(f32[5,256,512]{2,1,0:T(8,128)S(1)} %copy-done.10, ...), kind=kLoop, calls=%fused_computation.172 | loop fusion | flops 13104128 | bytes 23624704 | tf_op jit(solution)/shard_map/transpose(jvp())/reduce_sum | solution.py:16
  387.4 4.4 convolution_add_fusion.10
  391.9 4.0 convolution_add_fusion.9
  396.0 0.9 copy.27
  397.1 7.0 convolution_add_fusion.8
  404.2 1.2 copy-done.33
  405.5 4.6 fusion.74
  410.1 2.3 convolution_add_fusion.13
  412.6 2.2 convolution_add_fusion.12
  415.1 4.1 convolution_add_fusion.11
  419.3 37.4 %all-reduce.72 = (f32[512]{0:T(512)S(1)}, f32[512]{0:T(512)S(1)}, f32[512]{0:T(512)S(1)}, f32[1536]{0:T(1024)S(1)}, f32[512]{0:T(512)S(1)}, /*index=5*/f32[512]{0:T(512)S(1)}) all-reduce(f32[512]{0:T(512)S(1)} %add_add_fusion.10, f32[512]{0:T(512)S(1)} %add_add_fusion.9, ...), channel_id=3, replica_groups=mesh['dp'=4,'fsdp'=8] {'dp','fsdp'}, use_global_device_ids=true, to_apply=%region_49.50.clone | all-reduce | flops 4096 | bytes 32768
  460.2 5.3 add_convert_fusion.6
  465.5 15.9 %fusion.40 = (bf16[5,256,512]{2,1,0:T(8,128)(2,1)S(1)}, bf16[5,256,512]{2,1,0:T(8,128)(2,1)}) fusion(f32[5,256,512]{2,1,0:T(8,128)} %get-tuple-element.144, f32[5,256,512]{2,1,0:T(8,128)} %get-tuple-element.143, f32[5,256,512]{2,1,0:T(8,128)} %get-tuple-element.141, f32[5,256,512]{2,1,0:T(8,128)} %get-tuple-element.142, ...), kind=kLoop, calls=%fused_computation.116 | loop fusion | flops 11796480 | bytes 41943040 | tf_op jit(solution)/shard_map/convert_element_type | solution.py:141
  481.5 14.4 %fusion.41 = (bf16[5,256,512]{2,1,0:T(8,128)(2,1)}, bf16[5,256,512]{2,1,0:T(8,128)(2,1)}) fusion(f32[5,256,512]{2,1,0:T(8,128)} %get-tuple-element.151, f32[5,256,512]{2,1,0:T(8,128)} %get-tuple-element.150, f32[5,256,512]{2,1,0:T(8,128)} %get-tuple-element.148, f32[5,256,512]{2,1,0:T(8,128)} %get-tuple-element.149, f32[5,256,512]{2,1,0:T(8,128)} %get-tuple-element.146, ...), kind=kLoop, calls=%fused_computation.117 | loop fusion | flops 11796480 | bytes 41943040 | tf_op jit(solution)/shard_map/convert_element_type | solution.py:141
  495.9 6.4 pad_maximum_fusion.1
  502.3 3.0 pad_maximum_fusion
  505.2 24.7 %reduce-scatter.10.cloned.1.call-done = f32[16,7]{1,0:T(8,128)} async-done(((f32[512,7]{1,0:T(8,128)}), f32[16,7]{1,0:T(8,128)}) %reduce-scatter.10.cloned.1.call-update) | async-done | bytes 464
  529.9 1.4 copy.28
  531.3 103.0 %reduce-scatter.8.cloned.1.call-done = f32[48,512]{1,0:T(8,128)} async-done(((f32[1536,512]{1,0:T(8,128)}), f32[48,512]{1,0:T(8,128)}) %reduce-scatter.8.cloned.1.call-update) | async-done | bytes 98320 | tf_op jit(solution)/shard_map/reduce_scatter | solution.py:161
  634.3 107.0 %reduce-scatter.6.cloned.1.call-done = f32[16,1536]{1,0:T(8,128)} async-done(((f32[512,1536]{1,0:T(8,128)}), f32[16,1536]{1,0:T(8,128)}) %reduce-scatter.6.cloned.1.call-update) | async-done | bytes 98320 | tf_op jit(solution)/shard_map/reduce_scatter | solution.py:159
  (255 shorter events, 7.6 us)
Async XLA Ops:
  7.2 164.1 %all-gather.4.cloned.1.call-start = ((), (), s32[]{:S(2)}) async-start(), calls=%async_computation.3 | async-start | bytes 1622016 | tf_op jit(solution)/shard_map/all_gather | solution.py:74
  7.9 206.9 %all-gather.6.cloned.1.call-start = ((), (), s32[]{:S(2)}) async-start(), calls=%async_computation.4 | async-start | bytes 1622016 | tf_op jit(solution)/shard_map/all_gather | solution.py:76
  8.7 521.3 %reduce-scatter.10.cloned.1.call-start = ((), (), s32[]{:S(2)}) async-start(), calls=%async_computation.7 | async-start | bytes 270336
  123.1 7.2 copy-start.56
  123.1 7.2 copy-start.66
  123.2 7.2 copy-start.68
  123.2 7.2 copy-start.70
  123.2 7.2 copy-start.72
  123.2 7.2 copy-start.74
  123.2 7.2 copy-start.76
  158.7 8.8 %copy-start = (f32[5,256,512]{2,1,0:T(8,128)}, f32[5,256,512]{2,1,0:T(8,128)S(1)}, u32[]{:S(2)}) copy-start(f32[5,256,512]{2,1,0:T(8,128)S(1)} %get-tuple-element.92) | copy-start | bytes 7864324
  158.7 8.8 %copy-start.2 = (f32[5,256,512]{2,1,0:T(8,128)}, f32[5,256,512]{2,1,0:T(8,128)S(1)}, u32[]{:S(2)}) copy-start(f32[5,256,512]{2,1,0:T(8,128)S(1)} %get-tuple-element.168) | copy-start | bytes 7864324
  158.8 8.8 %copy-start.4 = (f32[5,256,512]{2,1,0:T(8,128)}, f32[5,256,512]{2,1,0:T(8,128)S(1)}, u32[]{:S(2)}) copy-start(f32[5,256,512]{2,1,0:T(8,128)S(1)} %get-tuple-element.170) | copy-start | bytes 7864324
  158.8 8.8 %copy-start.6 = (f32[5,256,512]{2,1,0:T(8,128)}, f32[5,256,512]{2,1,0:T(8,128)S(1)}, u32[]{:S(2)}) copy-start(f32[5,256,512]{2,1,0:T(8,128)S(1)} %get-tuple-element.172) | copy-start | bytes 7864324
  158.8 8.8 %copy-start.46 = (f32[5,256]{1,0:T(8,128)}, f32[5,256]{1,0:T(8,128)S(1)}, u32[]{:S(2)}) copy-start(f32[5,256]{1,0:T(8,128)S(1)} %broadcast_multiply_fusion.28) | copy-start | bytes 15364
  158.8 8.8 %copy-start.40 = (f32[5,256]{1,0:T(8,128)}, f32[5,256]{1,0:T(8,128)S(1)}, u32[]{:S(2)}) copy-start(f32[5,256]{1,0:T(8,128)S(1)} %broadcast_multiply_fusion.29) | copy-start | bytes 15364
  159.8 7.8 %copy-start.48 = (f32[5,256]{1,0:T(8,128)}, f32[5,256]{1,0:T(8,128)S(1)}, u32[]{:S(2)}) copy-start(f32[5,256]{1,0:T(8,128)S(1)} %fusion.50) | copy-start | bytes 15364
  160.8 6.8 copy-start.54
  160.8 6.7 copy-start.42
  160.9 6.7 copy-start.44
  162.7 5.0 copy-start.50
  162.7 4.9 copy-start.52
  162.7 4.9 copy-start.78
  171.3 22.9 %copy-start.23 = (bf16[5,256,512]{2,1,0:T(8,128)(2,1)S(1)}, bf16[5,256,512]{2,1,0:T(8,128)(2,1)}, u32[]{:S(2)}) copy-start(bf16[5,256,512]{2,1,0:T(8,128)(2,1)} %get-tuple-element.183) | copy-start | bytes 3932164
  171.3 22.9 %copy-start.86 = (bf16[512,1536]{1,0:T(8,128)(2,1)S(1)}, bf16[512,1536]{1,0:T(8,128)(2,1)}, u32[]{:S(2)}) copy-start(bf16[512,1536]{1,0:T(8,128)(2,1)} %all-gather.4.cloned.1.call-done) | copy-start | bytes 4718596
  214.8 5.0 copy-start.87
  214.8 5.0 copy-start.89
  222.0 45.3 %copy-start.14 = (f32[1280,512]{1,0:T(8,128)}, f32[1280,512]{1,0:T(8,128)S(1)}, u32[]{:S(2)}) copy-start(f32[1280,512]{1,0:T(8,128)S(1)} %convolution_add_fusion.4) | copy-start | bytes 7864324
  242.4 24.9 %slice-start = ((s8[5242880]{0:T(1024)(128)(4,1)}), s8[4194304]{0:T(1024)(128)(4,1)S(1)}, s32[]{:S(2)}) async-start(s8[5242880]{0:T(1024)(128)(4,1)} %bitcast.107), calls=%async_computation.8 | async-start | bytes 8388608
  244.7 22.7 %slice-start.1 = ((s8[5242880]{0:T(1024)(128)(4,1)}), s8[1048576]{0:T(1024)(128)(4,1)S(1)}, s32[]{:S(2)}) async-start(s8[5242880]{0:T(1024)(128)(4,1)} %bitcast.107), calls=%async_computation.9 | async-start | bytes 2097152
  265.1 4.8 slice-start.3
  265.1 4.8 copy-start.80
  265.1 4.8 copy-start.82
  265.1 4.8 copy-start.83
  265.1 4.8 copy-start.84
  265.1 4.8 copy-start.85
  267.4 7.6 %copy-start.16 = (f32[1280,512]{1,0:T(8,128)}, f32[1280,512]{1,0:T(8,128)S(1)}, u32[]{:S(2)}) copy-start(f32[1280,512]{1,0:T(8,128)S(1)} %convolution_add_fusion.5) | copy-start | bytes 7864324
  275.0 7.5 copy-start.34
  275.0 19.4 %copy-start.38 = (bf16[5,256,512]{2,1,0:T(8,128)(2,1)}, bf16[5,256,512]{2,1,0:T(8,128)(2,1)S(1)}, u32[]{:S(2)}) copy-start(bf16[5,256,512]{2,1,0:T(8,128)(2,1)S(1)} %get-tuple-element.126) | copy-start | bytes 3932164
  275.0 29.5 %copy-start.36 = (bf16[5,256,512]{2,1,0:T(8,128)(2,1)}, bf16[5,256,512]{2,1,0:T(8,128)(2,1)S(1)}, u32[]{:S(2)}) copy-start(bf16[5,256,512]{2,1,0:T(8,128)(2,1)S(1)} %get-tuple-element.124) | copy-start | bytes 3932164
  275.0 7.4 copy-start.88
  324.0 4.7 copy-start.41
  324.0 4.7 copy-start.43
  324.0 4.7 copy-start.45
  324.0 4.7 copy-start.49
  324.0 4.7 copy-start.51
  337.3 8.1 %copy-start.9 = (f32[5,256,512]{2,1,0:T(8,128)}, f32[5,256,512]{2,1,0:T(8,128)S(1)}, u32[]{:S(2)}) copy-start(f32[5,256,512]{2,1,0:T(8,128)S(1)} %get-tuple-element.82) | copy-start | bytes 7864324
  364.2 15.1 %copy-start.8 = (f32[5,256,512]{2,1,0:T(8,128)S(1)}, f32[5,256,512]{2,1,0:T(8,128)}, u32[]{:S(2)}) copy-start(f32[5,256,512]{2,1,0:T(8,128)} %get-tuple-element.191) | copy-start | bytes 7864324
  364.2 15.1 %copy-start.10 = (f32[5,256,512]{2,1,0:T(8,128)S(1)}, f32[5,256,512]{2,1,0:T(8,128)}, u32[]{:S(2)}) copy-start(f32[5,256,512]{2,1,0:T(8,128)} %get-tuple-element.136) | copy-start | bytes 7864324
  379.4 8.0 %copy-start.39 = (bf16[5,256,512]{2,1,0:T(8,128)(2,1)S(1)}, bf16[5,256,512]{2,1,0:T(8,128)(2,1)}, u32[]{:S(2)}) copy-start(bf16[5,256,512]{2,1,0:T(8,128)(2,1)} %copy-done.38) | copy-start | bytes 3932164
  379.4 8.0 %copy-start.90 = (bf16[1280,1536]{1,0:T(8,128)(2,1)S(1)}, bf16[1280,1536]{1,0:T(8,128)(2,1)}, u32[]{:S(2)}) copy-start(bf16[1280,1536]{1,0:T(8,128)(2,1)} %get-tuple-element.93) | copy-start | bytes 11796484
  391.9 5.3 copy-start.35
  396.9 237.4 %reduce-scatter.8.cloned.1.call-start = ((), (), s32[]{:S(2)}) async-start(), calls=%async_computation.6 | async-start | bytes 3244032 | tf_op jit(solution)/shard_map/reduce_scatter | solution.py:161
  404.2 5.9 copy-start.27
  404.2 337.1 %reduce-scatter.6.cloned.1.call-start = ((), (), s32[]{:S(2)}) async-start(), calls=%async_computation.5 | async-start | bytes 3244032 | tf_op jit(solution)/shard_map/reduce_scatter | solution.py:159
  419.1 41.0 %copy-start.15 = (f32[1280,512]{1,0:T(8,128)S(1)}, f32[1280,512]{1,0:T(8,128)}, u32[]{:S(2)}) copy-start(f32[1280,512]{1,0:T(8,128)} %copy-done.14) | copy-start | bytes 7864324
  460.2 21.2 %slice-start.4 = ((s8[5242880]{0:T(1024)(128)(4,1)}), s8[4194304]{0:T(1024)(128)(4,1)S(1)}, s32[]{:S(2)}) async-start(s8[5242880]{0:T(1024)(128)(4,1)} %bitcast.111), calls=%async_computation.12 | async-start | bytes 8388608
  465.5 16.0 %slice-start.5 = ((s8[5242880]{0:T(1024)(128)(4,1)}), s8[1048576]{0:T(1024)(128)(4,1)S(1)}, s32[]{:S(2)}) async-start(s8[5242880]{0:T(1024)(128)(4,1)} %bitcast.111), calls=%async_computation.13 | async-start | bytes 2097152
  465.5 16.0 %copy-start.12 = (f32[5,256,512]{2,1,0:T(8,128)S(1)}, f32[5,256,512]{2,1,0:T(8,128)}, u32[]{:S(2)}) copy-start(f32[5,256,512]{2,1,0:T(8,128)} %get-tuple-element.184) | copy-start | bytes 7864324
  465.5 16.0 %copy-start.13 = (f32[5,256,512]{2,1,0:T(8,128)S(1)}, f32[5,256,512]{2,1,0:T(8,128)}, u32[]{:S(2)}) copy-start(f32[5,256,512]{2,1,0:T(8,128)} %get-tuple-element.185) | copy-start | bytes 7864324
  495.8 6.4 copy-start.28
  495.9 6.4 copy-start.29
  495.9 6.4 copy-start.30
  495.9 6.4 copy-start.31
  (41 other events, 131.2 us)
Sparse Core Ops, SparseCore 0:
  10.9 57.7 all-gather.3
  71.6 53.9 all-gather.5
  397.0 132.8 reduce-scatter.9
  535.8 98.4 reduce-scatter.7
  640.1 101.0 reduce-scatter.5
where the time goes:
time: 758 us; the launch traced here: 748 us
  waiting for transfers between devices  236 us (31%)
  matrix products  176 us (23%)
  other arithmetic  155 us (20%)
  blocking collectives  146 us (19%)
  local copies, waits for them, and re-layouts  19 us (3%)
  between operations  15.7 us (2%)
    reduce_scatter x1, waiting for transfers between devices, on_device(): lax.psum_scatter(totals[4], ('dp', 'fsdp'), scatter_dimension=0, tiled=True)  107 us
    reduce_scatter x1, waiting for transfers between devices, on_device(): lax.psum_scatter(totals[6], ('dp', 'fsdp'), scatter_dimension=0, tiled=True)  103 us
    dot_general x4, matrix products, on_device(): jnp.dot(rows_low, full_in, preferred_element_type=jnp.float32)  84.2 us
    unnamed x2, blocking collectives  79.6 us
    all_gather x1, blocking collectives, on_device(): lax.all_gather(conv_weight, ('dp', 'fsdp'), axis=0, tiled=True)  66.8 us
    reduce_sum x4, other arithmetic, conv_norm(): padded[:, offset:offset + frames, :] * conv_weight[:, offset]  50 us
    dot_general x8, matrix products, contract_last(): lax.dot_general(left_side, right_side, (((1,), (1,)), ((), ())), preferre...  44.2 us
    dot_general x8, matrix products, contract_rows(): lax.dot_general(left_side, right_side, (((0,), (0,)), ((), ())), preferre...  36 us
  transfers between devices with their start and end apart: 5, of which 3 were waited for; matrix products, arithmetic and copies ran while one was open for 22% of the time, Pallas kernels for 0%

commit v1 on v0

v1 whole, which is shorter than its diff:
```python
from functools import partial
import jax
import jax.numpy as jnp
from jax import lax
from jax.experimental import pallas as pl
from jax.experimental.pallas import tpu as pltpu
from jax.sharding import PartitionSpec as P

F32 = jnp.float32
BF16 = jnp.bfloat16
PAD = 8
ROOT_HALF = 0.7071067811865476
LOG2E = 1.4426950408889634
INV_ROOT_2PI = 0.3989422804014327


def dot_nn(a, b):
    return lax.dot_general(a, b, (((1,), (0,)), ((), ())), preferred_element_type=F32)


def dot_nt(a, b):
    return lax.dot_general(a, b, (((1,), (1,)), ((), ())), preferred_element_type=F32)


def fold8(v):
    total = v[0:8]
    for r in range(8, v.shape[0], 8):
        total = total + v[r : r + 8]
    return total


def clip_kernel(
    live_ref,
    x_ref,
    dy_ref,
    w_in_ref,
    w_out_ref,
    rows_ref,
    ib_ref,
    out_ref,
    gx_ref,
    gin_ref,
    gout_ref,
    small_ref,
    gib_ref,
    xp,
    gm,
    xh,
    rs,
    nb,
    nbt,
    gob,
    gobt,
    ab,
    ghb,
    gn,
    acc_in,
    acc_out,
    acc_small,
    acc_ib,
    *,
    taps,
    hid_chunk,
    row_chunk,
):
    step = pl.program_id(0)
    frames, chans = xh.shape
    hid = ab.shape[1]
    margin = (taps - 1) // 2

    @pl.when(step == 0)
    def _():
        acc_in[...] = jnp.zeros_like(acc_in)
        acc_out[...] = jnp.zeros_like(acc_out)
        acc_small[...] = jnp.zeros_like(acc_small)
        acc_ib[...] = jnp.zeros_like(acc_ib)
        xp[0:PAD, :] = jnp.zeros((PAD, chans), F32)
        xp[PAD + frames :, :] = jnp.zeros((PAD, chans), F32)
        gm[0:PAD, :] = jnp.zeros((PAD, chans), F32)
        gm[PAD + frames :, :] = jnp.zeros((PAD, chans), F32)

    live = live_ref[step] != 0

    @pl.when(jnp.logical_not(live))
    def _():
        out_ref[...] = x_ref[...]
        gx_ref[...] = dy_ref[...]

    @pl.when(live)
    def _():
        def row(i):
            return rows_ref[i : i + 1, :]

        for r in range(0, frames, row_chunk):
            xp[PAD + r : PAD + r + row_chunk, :] = x_ref[0, r : r + row_chunk, :].astype(F32)
        for r in range(0, frames, row_chunk):
            base = PAD - margin + r
            mixed = row(taps) + xp[base : base + row_chunk, :] * row(0)
            for k in range(1, taps):
                mixed = mixed + xp[base + k : base + k + row_chunk, :] * row(k)
            center = mixed - jnp.mean(mixed, axis=-1, keepdims=True)
            var = jnp.mean(center * center, axis=-1, keepdims=True)
            inv = lax.rsqrt(var + 1e-06)
            xhat = center * inv
            xh[r : r + row_chunk, :] = xhat
            rs[r : r + row_chunk, :] = jnp.broadcast_to(inv, (row_chunk, 128))
            nb[r : r + row_chunk, :] = (xhat * row(taps + 1) + row(taps + 2)).astype(BF16)
            go = (dy_ref[0, r : r + row_chunk, :].astype(F32) * row(taps + 4)).astype(BF16)
            gob[r : r + row_chunk, :] = go
            acc_small[taps + 3, :, :] += fold8(go.astype(F32))
        nbt[...] = nb[...].T
        gobt[...] = gob[...].T

        for j in range(0, hid, hid_chunk):
            cols = slice(j, j + hid_chunk)
            h = dot_nn(nb[...], w_in_ref[:, cols]) + ib_ref[0:1, cols]
            u = h * ROOT_HALF
            cdf = 0.5 * lax.erf(u) + 0.5
            slope = cdf + h * (jnp.exp2(u * u * (-LOG2E)) * INV_ROOT_2PI)
            ab[:, cols] = (h * cdf).astype(BF16)
            ga = dot_nt(gob[...], w_out_ref[cols, :])
            gh = (ga * slope).astype(BF16)
            ghb[:, cols] = gh
            acc_ib[:, cols] += fold8(gh.astype(F32))
        gn[...] = dot_nt(ghb[...], w_in_ref[...])
        output = dot_nn(ab[...], w_out_ref[...]) + row(taps + 3)
        for r in range(0, frames, row_chunk):
            o = output[r : r + row_chunk, :]
            dy = dy_ref[0, r : r + row_chunk, :].astype(F32)
            acc_small[taps + 4, :, :] += fold8(dy * o)
            x = x_ref[0, r : r + row_chunk, :].astype(F32)
            out_ref[0, r : r + row_chunk, :] = (x + o * row(taps + 4)).astype(BF16)
        for j in range(0, hid, hid_chunk):
            cols = slice(j, j + hid_chunk)
            acc_out[:, cols] += dot_nn(gobt[...], ab[:, cols])
            acc_in[:, cols] += dot_nn(nbt[...], ghb[:, cols])

        for r in range(0, frames, row_chunk):
            g = gn[r : r + row_chunk, :]
            xhat = xh[r : r + row_chunk, :]
            gxh = g * xhat
            acc_small[taps + 2, :, :] += fold8(g)
            acc_small[taps + 1, :, :] += fold8(gxh)
            gg = g * row(taps + 1)
            m1 = jnp.mean(gg, axis=-1, keepdims=True)
            m2 = jnp.mean(gg * xhat, axis=-1, keepdims=True)
            gmix = rs[r : r + row_chunk, 0:1] * (gg - m1 - xhat * m2)
            acc_small[taps, :, :] += fold8(gmix)
            gm[PAD + r : PAD + r + row_chunk, :] = gmix
        for r in range(0, frames, row_chunk):
            base = PAD + margin + r
            x = xp[PAD + r : PAD + r + row_chunk, :]
            total = dy_ref[0, r : r + row_chunk, :].astype(F32)
            for k in range(taps):
                shifted = gm[base - k : base - k + row_chunk, :]
                total = total + shifted * row(k)
                acc_small[k, :, :] += fold8(shifted * x)
            gx_ref[0, r : r + row_chunk, :] = total.astype(BF16)

    @pl.when(step == pl.num_programs(0) - 1)
    def _():
        gin_ref[...] = acc_in[...].astype(gin_ref.dtype)
        for j in range(0, hid, 128):
            gout_ref[j : j + 128, :] = acc_out[:, j : j + 128].T.astype(gout_ref.dtype)
        small_ref[...] = acc_small[...]
        gib_ref[...] = acc_ib[...]


def clip_call(live, x, dy, w_in, w_out, rows, ib, taps, grad_dtype=F32):
    clips, frames, chans = x.shape
    hid = w_in.shape[1]
    clip_spec = pl.BlockSpec((1, frames, chans), lambda i, live: (i, 0, 0))
    whole = lambda shape: pl.BlockSpec(shape, lambda i, live: (0,) * len(shape), pipeline_mode=pl.Buffered(1))
    kinds = taps + 5
    return pl.pallas_call(
        partial(clip_kernel, taps=taps, hid_chunk=256, row_chunk=32),
        out_shape=(
            jax.ShapeDtypeStruct(x.shape, BF16),
            jax.ShapeDtypeStruct(x.shape, BF16),
            jax.ShapeDtypeStruct((chans, hid), grad_dtype),
            jax.ShapeDtypeStruct((hid, chans), grad_dtype),
            jax.ShapeDtypeStruct((kinds, 8, chans), F32),
            jax.ShapeDtypeStruct((8, hid), F32),
        ),
        grid_spec=pltpu.PrefetchScalarGridSpec(
            num_scalar_prefetch=1,
            grid=(clips,),
            in_specs=[
                clip_spec,
                clip_spec,
                whole((chans, hid)),
                whole((hid, chans)),
                whole(rows.shape),
                whole(ib.shape),
            ],
            out_specs=(
                clip_spec,
                clip_spec,
                whole((chans, hid)),
                whole((hid, chans)),
                whole((kinds, 8, chans)),
                whole((8, hid)),
            ),
            scratch_shapes=[
                pltpu.VMEM((frames + 2 * PAD, chans), F32),
                pltpu.VMEM((frames + 2 * PAD, chans), F32),
                pltpu.VMEM((frames, chans), F32),
                pltpu.VMEM((frames, 128), F32),
                pltpu.VMEM((frames, chans), BF16),
                pltpu.VMEM((chans, frames), BF16),
                pltpu.VMEM((frames, chans), BF16),
                pltpu.VMEM((chans, frames), BF16),
                pltpu.VMEM((frames, hid), BF16),
                pltpu.VMEM((frames, hid), BF16),
                pltpu.VMEM((frames, chans), F32),
                pltpu.VMEM((chans, hid), F32),
                pltpu.VMEM((chans, hid), F32),
                pltpu.VMEM((kinds, 8, chans), F32),
                pltpu.VMEM((8, hid), F32),
            ],
        ),
        compiler_params=pltpu.CompilerParams(vmem_limit_bytes=56 << 20),
        name="clips",
    )(live, x, dy, w_in, w_out, rows, ib)


def on_device(
    mel_clips,
    live_counts,
    conv_weight,
    conv_bias,
    norm_gain,
    norm_shift,
    in_weight,
    in_bias,
    out_weight,
    out_bias,
    layer_scale,
    cotangent,
):
    axes = ("dp", "fsdp")
    taps = conv_weight.shape[1]
    micro_count = live_counts.shape[1]
    slot_count = mel_clips.shape[0] // micro_count
    gather = partial(lax.all_gather, axis_name=axes, axis=0, tiled=True)
    scatter = partial(lax.psum_scatter, axis_name=axes, scatter_dimension=0, tiled=True)

    full_in = gather(in_weight)
    full_out = gather(out_weight)
    columns = jnp.stack([conv_bias, norm_gain, norm_shift, out_bias, layer_scale], axis=1)
    rows = gather(jnp.concatenate([conv_weight, columns], axis=1)).T.astype(F32)
    rows = jnp.pad(rows, ((0, 16 - rows.shape[0]), (0, 0)))
    bias_row = jnp.broadcast_to(gather(in_bias).astype(F32), (8, full_in.shape[1]))
    live = (lax.iota(jnp.int32, slot_count)[None, :] < live_counts[0][:, None]).astype(jnp.int32)

    block_out, grad_clips, grad_in, grad_out, small, grad_ib = clip_call(
        live.reshape(-1), mel_clips, cotangent, full_in, full_out, rows, bias_row, taps
    )
    small = scatter(jnp.sum(small, axis=1).T)
    return (
        block_out,
        grad_clips,
        small[:, :taps],
        small[:, taps],
        small[:, taps + 1],
        small[:, taps + 2],
        scatter(grad_in),
        scatter(jnp.sum(grad_ib, axis=0)),
        scatter(grad_out),
        small[:, taps + 3],
        small[:, taps + 4],
    )


def solution(mesh):
    both = ("dp", "fsdp")
    row, mat, cube = P(both), P(both, None), P(both, None, None)
    in_specs = (cube, mat, mat, row, row, row, mat, row, mat, row, row, cube)
    out_specs = (cube, cube, mat, row, row, row, mat, row, mat, row, row)
    return jax.shard_map(on_device, mesh=mesh, in_specs=in_specs, out_specs=out_specs, check_vma=False)
```

time: 758 us -> 579 us (0.76)
  matrix products: 176 us -> 0 us
  other arithmetic: 155 us -> 2.37 us
  Pallas kernels: 0 us -> 81.2 us
  waiting for transfers between devices: 236 us -> 305 us
  blocking collectives: 146 us -> 157 us
    dot_general x24 -> x0, matrix products: 176 us -> none  [the longest x4 84.2 us: on_device(): jnp.dot(rows_low, full_in, preferred_element_type=jnp.float32)]
    reduce_sum x10 -> x2, other arithmetic: 89.4 us -> 1.01 us  [the longest x1 0.99 us: on_device(): small = scatter(jnp.sum(small, axis=1).T)]
    pallas_call x0 -> x1, Pallas kernels: none -> 81.2 us  [clip_call(): pl.pallas_call(partial(clip_kernel, taps=taps, hid_chunk=256, row_chunk=3...]
    unnamed x6, waiting for transfers between devices: 26.1 us -> 96.5 us
    convert_element_type x14 -> x1, other arithmetic: 55.6 us -> 0.74 us  [on_device(): (lax.iota(jnp.int32, slot_count)[None, :] < live_counts[0][:, None]).asty...]
    unnamed x220 -> x13, local copies, waits for them, and re-layouts: 18.1 us -> 7.34 us
    concatenate x2 -> x0, other arithmetic: 9.33 us -> none  [the longest x1 6.37 us: on_device(): grad_clips = jnp.concatenate(block_grads, axis=0)]
  transfers between devices with their start and end apart: 5 -> 5, of which waited for: 3 -> 4; matrix products, arithmetic and copies ran while one was open for 22% -> 2% of each run, Pallas kernels for 0% -> 0%
where the time goes in v1:
time: 579 us; the launch traced here: 573 us
  waiting for transfers between devices  305 us (53%)
  blocking collectives  157 us (27%)
  Pallas kernels  81.2 us (14%)
  between operations  13.8 us (2%)
  local copies, waits for them, and re-layouts  13.4 us (2%)
    reduce_scatter x1, waiting for transfers between devices, on_device(): scatter(grad_out)  107 us
    reduce_scatter x1, waiting for transfers between devices, on_device(): scatter(grad_in)  99.5 us
    unnamed x6, waiting for transfers between devices  96.5 us
    unnamed x2, blocking collectives  86.8 us
    pallas_call x1, Pallas kernels, clip_call(): pl.pallas_call(partial(clip_kernel, taps=taps, hid_chunk=256, row_chunk=3...  81.2 us
    all_gather x1, blocking collectives, on_device(): rows = gather(jnp.concatenate([conv_weight, columns], axis=1)).T.astype(F32)  70.6 us
  transfers between devices with their start and end apart: 5, of which 4 were waited for; matrix products, arithmetic and copies ran while one was open for 2% of the time, Pallas kernels for 0%

profile of v1, /device:TPU:0, one launch (start us, length us, event | category | flops | bytes accessed | tf_op | source)
XLA Modules:
  0.0 573.4 jit_solution(15411053570009783309)
XLA Ops:
  7.2 0.0 all-gather.3.cloned.1.call-start
  7.2 0.7 all-gather.3.cloned.1.call-update
  7.9 0.0 all-gather.5.cloned.1.call-start
  8.0 0.7 all-gather.5.cloned.1.call-update
  8.7 0.0 reduce-scatter.10.cloned.1.call-start
  8.7 0.8 copy.23
  9.5 0.7 copy.24
  10.2 0.7 copy.25
  11.0 0.7 copy.26
  11.7 0.7 copy.27
  12.5 0.7 copy.28
  13.2 0.1 concatenate.3
  13.3 70.6 %all_gather.14 = bf16[512,12]{1,0:T(8,128)(2,1)S(1)} all-gather(bf16[16,12]{1,0:T(8,128)(2,1)S(1)} %concatenate.3), channel_id=1, replica_groups=mesh['dp'=4,'fsdp'=8] {'dp','fsdp'}, dimensions={0}, use_global_device_ids=true | all-gather | bytes 12672 | tf_op jit(solution)/shard_map/all_gather | solution.py:251
  83.9 0.1 copy.29
  84.0 0.7 fusion
  84.7 0.6 reshape.29.live_ref
  85.3 0.8 dynamic-update-slice
  86.2 37.0 %all-reduce.1 = bf16[1536]{0:T(1024)(128)(2,1)S(1)} all-reduce(bf16[1536]{0:T(1024)(128)(2,1)S(1)} %dynamic-update-slice), channel_id=1, replica_groups=mesh['dp'=4,'fsdp'=8] {'dp','fsdp'}, use_global_device_ids=true, to_apply=%add.1 | all-reduce | flops 1536 | bytes 6144
  123.2 0.6 pad_convert_fusion.rows_ref
  123.8 0.0 all-gather.3.cloned.1.call-done.w_in_ref
  123.8 2.0 all-gather.5.cloned.1.call-done.w_out_ref
  125.8 0.6 broadcast_in_dim.4.ib_ref
  126.4 81.2 %clips.1 = (bf16[20,256,512]{2,1,0:T(8,128)(2,1)}, bf16[20,256,512]{2,1,0:T(8,128)(2,1)}, f32[512,1536]{1,0:T(8,128)}, f32[1536,512]{1,0:T(8,128)}, f32[12,8,512]{2,1,0:T(8,128)}, /*index=5*/f32[8,1536]{1,0:T(8,128)}) custom-call(s32[20]{0:T(128)} %reshape.29.live_ref, bf16[20,256,512]{2,1,0:T(8,128)(2,1)} %x_ref.1, bf16[20,256,512]{2,1,0:T(8,128)(2,1)} %dy_ref.1, ...), custom_call_target="tpu_custom_call" | custom-call | tf_op jit(solution)/shard_map/clips/pallas_call | solution.py:175
  207.6 0.0 copy-start
  207.6 1.0 reduce_sum.18
  208.6 0.9 copy.30
  209.4 0.0 reduce-scatter.10.cloned.1.call-update
  209.5 0.0 reduce-scatter.6.cloned.1.call-start
  209.5 0.5 reduce-scatter.6.cloned.1.call-update
  210.0 0.0 reduce-scatter.8.cloned.1.call-start
  210.1 0.5 reduce-scatter.8.cloned.1.call-update
  210.6 0.0 copy-done
  210.7 49.8 %all-reduce.2 = f32[1536]{0:T(1024)S(1)} all-reduce(f32[1536]{0:T(1024)S(1)} %reduce_sum.19), channel_id=4, replica_groups=mesh['dp'=4,'fsdp'=8] {'dp','fsdp'}, use_global_device_ids=true, to_apply=%region_4.5.clone | all-reduce | flops 1536 | bytes 12288
  260.4 0.6 dynamic-slice
  261.0 94.0 %reduce-scatter.10.cloned.1.call-done = f32[16,12]{1,0:T(8,128)} async-done(((f32[512,12]{1,0:T(8,128)}), f32[16,12]{1,0:T(8,128)}) %reduce-scatter.10.cloned.1.call-update) | async-done | bytes 784
  355.1 1.0 fusion.1
  356.0 0.6 copy.34
  356.6 0.6 copy.35
  357.2 0.6 copy.36
  357.8 0.6 copy.37
  358.4 0.6 copy.33
  358.9 1.4 copy.32
  360.3 99.5 %reduce-scatter.6.cloned.1.call-done = f32[16,1536]{1,0:T(8,128)} async-done(((f32[512,1536]{1,0:T(8,128)}), f32[16,1536]{1,0:T(8,128)}) %reduce-scatter.6.cloned.1.call-update) | async-done | bytes 98320 | tf_op jit(solution)/shard_map/reduce_scatter | solution.py:267
  459.8 107.1 %reduce-scatter.8.cloned.1.call-done = f32[48,512]{1,0:T(8,128)} async-done(((f32[1536,512]{1,0:T(8,128)}), f32[48,512]{1,0:T(8,128)}) %reduce-scatter.8.cloned.1.call-update) | async-done | bytes 98320 | tf_op jit(solution)/shard_map/reduce_scatter | solution.py:269
  (2 shorter events, 0.0 us)
Async XLA Ops:
  7.2 116.6 %all-gather.3.cloned.1.call-start = ((), (), s32[]{:S(2)}) async-start(), calls=%async_computation.3 | async-start | bytes 1622016 | tf_op jit(solution)/shard_map/all_gather | solution.py:248
  7.9 117.9 %all-gather.5.cloned.1.call-start = ((), (), s32[]{:S(2)}) async-start(), calls=%async_computation.4 | async-start | bytes 1622016 | tf_op jit(solution)/shard_map/all_gather | solution.py:249
  8.7 346.4 %reduce-scatter.10.cloned.1.call-start = ((), (), s32[]{:S(2)}) async-start(), calls=%async_computation.7 | async-start | bytes 270336
  207.6 3.1 copy-start
  209.5 250.4 %reduce-scatter.6.cloned.1.call-start = ((), (), s32[]{:S(2)}) async-start(), calls=%async_computation.5 | async-start | bytes 3244032 | tf_op jit(solution)/shard_map/reduce_scatter | solution.py:267
  210.0 356.8 %reduce-scatter.8.cloned.1.call-start = ((), (), s32[]{:S(2)}) async-start(), calls=%async_computation.6 | async-start | bytes 3244032 | tf_op jit(solution)/shard_map/reduce_scatter | solution.py:269
Sparse Core Ops, SparseCore 0:
  10.9 57.8 all-gather.2
  71.6 54.0 all-gather.4
  209.6 145.4 reduce-scatter.9
  360.9 98.8 reduce-scatter.5
  465.7 101.1 reduce-scatter.7
